TPU v7x, 32 devices: a whole 2x2x4 slice. The times are simulated.
32 devices in a mesh: dp: 4 (over y, x), tensor: 8 (over z, core).
Axes of the slice: x: 2, y: 2, z: 4, core: 2. Of those that a mesh axis runs over, the one named last changes fastest.
Arguments:
- hidden_acts: bfloat16 [3, 1792, 14336], P(None, 'dp', 'tensor'), may hold values from -6 to 6
- out_grads: bfloat16 [3, 1792, 4096], P(None, 'dp', 'tensor'), may hold values from -6 to 6
Outputs:
- fisher: float32 [14336, 4096], P('tensor', 'dp')
All inputs are finite; a program needn't handle non-finite values.
Results may differ from a plain program's by a relative error of at most 0.018.
Values may be sent and summed in bfloat16 or wider, within the bound.
A program may use at most 128 MiB of HBM per device.

v0:
```python
import math

import jax
import jax.numpy as jnp
import numpy as np
from jax import lax
from jax.sharding import PartitionSpec as P

FF = 14336
FACTOR_A = 28
SEQS = 3


def sylvester(order):
    result = np.ones((1, 1))
    for doubling in range(order.bit_length() - 1):
        result = np.kron(result, np.array([[1.0, 1.0], [1.0, -1.0]]))
    return result


def paley_matrix():
    residues = set((number * number % 13 for number in range(1, 13)))
    core_table = np.zeros((14, 14))
    core_table[0, 1:] = 1.0
    core_table[1:, 0] = 1.0
    for row_index in range(13):
        for col_index in range(13):
            offset = (col_index - row_index) % 13
            if offset != 0:
                core_table[1 + row_index, 1 + col_index] = 1.0 if offset in residues else -1.0
    return np.kron(core_table, np.array([[1.0, 1.0], [1.0, -1.0]])) + np.kron(
        np.eye(14), np.array([[1.0, -1.0], [-1.0, -1.0]])
    )


def cross_rotate(values, scaling):
    tok_rows, local_ff = values.shape
    tensor_count = lax.axis_size("tensor")
    mixing = jnp.asarray(sylvester(tensor_count), jnp.float32)
    stacked = values.reshape(tok_rows, 1, local_ff)
    spread = lax.all_to_all(
        stacked.astype(jnp.bfloat16), "tensor", split_axis=0, concat_axis=1, tiled=True
    ).astype(stacked.dtype)
    mixed = jnp.einsum("tqc,qp->tpc", spread, mixing, precision=lax.Precision.HIGHEST)
    scaled = (mixed * scaling).astype(jnp.bfloat16)
    returned = lax.all_to_all(scaled, "tensor", split_axis=1, concat_axis=0, tiled=True)
    return returned.reshape(tok_rows, local_ff)


def on_device(hidden_acts, out_grads):
    seq_count, tok_rows, local_ff = hidden_acts.shape
    dp_count = lax.axis_size("dp")
    local_b = local_ff // FACTOR_A
    local_rot = jnp.asarray(np.kron(sylvester(local_b), paley_matrix()), jnp.bfloat16)
    scaling = 1.0 / math.sqrt(FF)
    inv_root = 1.0 / math.sqrt(tok_rows * dp_count)
    fisher = None
    for seq_index in range(seq_count):
        inner = jnp.dot(hidden_acts[seq_index], local_rot, preferred_element_type=jnp.float32)
        rotated = cross_rotate(inner, scaling)
        partial_sum = lax.dot_general(
            rotated,
            lax.all_gather(out_grads[seq_index], "tensor", axis=1, tiled=True),
            (((0,), (0,)), ((), ())),
            preferred_element_type=jnp.float32,
        )
        summed = lax.psum_scatter(
            partial_sum.astype(jnp.bfloat16), "dp", scatter_dimension=1, tiled=True
        ).astype(jnp.float32)
        gradient = summed * inv_root
        fisher = gradient * gradient if fisher is None else fisher + gradient * gradient
    return fisher / SEQS


def solution(mesh):
    placed = (P(None, "dp", "tensor"), P(None, "dp", "tensor"))
    return jax.shard_map(
        on_device, mesh=mesh, in_specs=placed, out_specs=P("tensor", "dp"), check_vma=False
    )
```

profile of v0, /device:TPU:0, one launch (start us, length us, event | category | flops | bytes accessed | tf_op | source)
XLA Modules:
  0.0 643.4 jit_solution(4570525206602376456)
XLA Ops:
  6.5 0.0 all-gather.7.cloned.1.call-start
  6.5 2.5 fusion.21
  9.0 0.0 all-gather.7.cloned.1.call-update
  9.0 0.0 all-gather.9.cloned.1.call-start
  9.1 0.7 all-gather.9.cloned.1.call-update
  9.8 6.4 fusion.3
  16.2 0.5 broadcast.17
  16.7 1.8 reduce.2
  18.5 1.9 reshape.29
  20.4 6.4 all-to-all-start
  26.7 0.0 all-gather.11.cloned.1.call-start
  26.8 0.7 all-gather.11.cloned.1.call-update
  27.5 0.0 reduce-scatter.4.cloned.1.call-start
  27.5 59.9 %all-to-all-done = bf16[8,2,50176]{2,1,0:T(2,128)(2,1)} async-done(((bf16[8,2,50176]{2,1,0:T(2,128)(2,1)}), bf16[8,2,50176]{2,1,0:T(2,128)(2,1)}, u32[]{:S(2)}, u32[]{:S(2)}) %all-to-all-start) | async-done | bytes 1605664 | tf_op jit(solution)/shard_map/all_to_all | solution.py:41
  87.4 4.7 reshape.30
  92.1 0.0 copy-start
  92.1 0.2 copy.31
  92.3 0.5 copy-done
  92.8 1.5 fusion.6
  94.3 0.3 copy.24
  94.6 63.7 %all_to_all.99 = bf16[56,8,1792]{2,0,1:T(8,128)(2,1)S(1)} all-to-all(bf16[56,8,1792]{2,0,1:T(8,128)(2,1)S(1)} %copy.24), channel_id=1, replica_groups=mesh['dp'=4,'tensor'=8] {'tensor'}, dimensions={1} | all-to-all | bytes 3211264 | tf_op jit(solution)/shard_map/all_to_all | solution.py:46
  158.3 0.0 all-gather.7.cloned.1.call-done
  158.3 13.1 %convolution_convert_fusion.2 = bf16[1792,4096]{1,0:T(8,128)(2,1)} fusion(bf16[448,1792]{1,0:T(8,128)(2,1)S(1)} %bitcast.82, bf16[1,448,4096]{2,1,0:T(8,128)(2,1)} %all-gather.7.cloned.1.call-done), kind=kOutput, calls=%fused_computation.2 | convolution fusion | flops 6584008704 | bytes 19955712 | tf_op jit(solution)/shard_map/dot_general | solution.py:61
  171.4 0.0 reduce-scatter.4.cloned.1.call-update
  171.5 0.2 reduce-scatter.6.cloned.1.call-start
  171.7 6.5 %fusion.4 = bf16[448,1,1792]{2,0,1:T(8,128)(2,1)S(1)} fusion(bf16[1792,1792]{1,0:T(8,128)(2,1)} %constant.11.clone, bf16[3,448,1792]{2,1,0:T(8,128)(2,1)} %param.6), kind=kOutput, calls=%fused_computation.14 | convolution fusion | flops 2878095360 | bytes 9633792 | tf_op jit(solution)/shard_map/dot_general | solution.py:59
  178.1 1.8 reduce.1
  180.0 0.5 reshape.27
  180.4 49.5 %all_to_all.100 = bf16[8,2,50176]{2,1,0:T(2,128)(2,1)} all-to-all(bf16[8,2,50176]{2,1,0:T(2,128)(2,1)S(1)} %reshape.27), channel_id=1, replica_groups=mesh['dp'=4,'tensor'=8] {'tensor'}, dimensions={0} | all-to-all | bytes 3211264 | tf_op jit(solution)/shard_map/all_to_all | solution.py:41
  229.9 4.6 reshape.28
  234.6 0.2 copy.32
  234.8 1.5 fusion.7
  236.3 0.3 copy.27
  236.6 40.9 %all_to_all.101 = bf16[56,8,1792]{2,0,1:T(8,128)(2,1)S(1)} all-to-all(bf16[56,8,1792]{2,0,1:T(8,128)(2,1)S(1)} %copy.27), channel_id=1, replica_groups=mesh['dp'=4,'tensor'=8] {'tensor'}, dimensions={1} | all-to-all | bytes 3211264 | tf_op jit(solution)/shard_map/all_to_all | solution.py:46
  277.5 0.0 all-gather.9.cloned.1.call-done
  277.5 13.1 %convolution_convert_fusion.1 = bf16[1792,4096]{1,0:T(8,128)(2,1)} fusion(bf16[448,1792]{1,0:T(8,128)(2,1)S(1)} %bitcast.83, bf16[1,448,4096]{2,1,0:T(8,128)(2,1)} %all-gather.9.cloned.1.call-done), kind=kOutput, calls=%fused_computation.1 | convolution fusion | flops 6584008704 | bytes 19955712 | tf_op jit(solution)/shard_map/dot_general | solution.py:61
  290.6 0.0 reduce-scatter.6.cloned.1.call-update
  290.6 0.3 reduce-scatter.8.cloned.1.call-start
  290.9 6.4 fusion.5
  297.3 1.8 reduce
  299.1 0.5 reshape.25
  299.6 41.6 %all_to_all.102 = bf16[8,2,50176]{2,1,0:T(2,128)(2,1)} all-to-all(bf16[8,2,50176]{2,1,0:T(2,128)(2,1)S(1)} %reshape.25), channel_id=1, replica_groups=mesh['dp'=4,'tensor'=8] {'tensor'}, dimensions={0} | all-to-all | bytes 3211264 | tf_op jit(solution)/shard_map/all_to_all | solution.py:41
  341.3 4.6 reshape.26
  345.8 0.2 copy.33
  346.0 1.5 fusion.8
  347.6 0.3 copy.30
  347.9 40.9 %all_to_all.103 = bf16[56,8,1792]{2,0,1:T(8,128)(2,1)S(1)} all-to-all(bf16[56,8,1792]{2,0,1:T(8,128)(2,1)S(1)} %copy.30), channel_id=1, replica_groups=mesh['dp'=4,'tensor'=8] {'tensor'}, dimensions={1} | all-to-all | bytes 3211264 | tf_op jit(solution)/shard_map/all_to_all | solution.py:46
  388.8 0.0 all-gather.11.cloned.1.call-done
  388.8 13.2 %convolution_convert_fusion = bf16[1792,4096]{1,0:T(8,128)(2,1)} fusion(bf16[448,1792]{1,0:T(8,128)(2,1)S(1)} %bitcast.84, bf16[1,448,4096]{2,1,0:T(8,128)(2,1)} %all-gather.11.cloned.1.call-done), kind=kOutput, calls=%fused_computation | convolution fusion | flops 6584008704 | bytes 19955712 | tf_op jit(solution)/shard_map/dot_general | solution.py:61
  401.9 0.0 reduce-scatter.8.cloned.1.call-update
  402.0 0.0 reduce-scatter.4.cloned.1.call-done
  402.0 86.3 %reduce-scatter.6.cloned.1.call-done = bf16[1792,1024]{1,0:T(8,128)(2,1)} async-done(((bf16[1792,4096]{1,0:T(8,128)(2,1)}), bf16[1792,1024]{1,0:T(8,128)(2,1)}) %reduce-scatter.6.cloned.1.call-update) | async-done | bytes 3670032 | tf_op jit(solution)/shard_map/reduce_scatter | solution.py:67
  488.3 140.7 %reduce-scatter.8.cloned.1.call-done = bf16[1792,1024]{1,0:T(8,128)(2,1)} async-done(((bf16[1792,4096]{1,0:T(8,128)(2,1)}), bf16[1792,1024]{1,0:T(8,128)(2,1)}) %reduce-scatter.8.cloned.1.call-update) | async-done | bytes 3670032 | tf_op jit(solution)/shard_map/reduce_scatter | solution.py:67
  629.0 7.5 %add_multiply_fusion = f32[1792,1024]{1,0:T(8,128)} fusion(bf16[1792,1024]{1,0:T(8,128)(2,1)} %reduce-scatter.8.cloned.1.call-done, bf16[1792,1024]{1,0:T(8,128)(2,1)} %reduce-scatter.6.cloned.1.call-done, bf16[1792,1024]{1,0:T(8,128)(2,1)} %reduce-scatter.4.cloned.1.call-done), kind=kLoop, calls=%fused_computation.3 | loop fusion | flops 22020096 | bytes 18350080 | tf_op jit(solution)/shard_map/div | solution.py:72
Async XLA Ops:
  6.5 151.8 %all-gather.7.cloned.1.call-start = ((), (), s32[]{:S(2)}) async-start(), calls=%async_computation.12 | async-start | bytes 4128768 | tf_op jit(solution)/shard_map/all_gather | solution.py:63
  9.0 268.5 %all-gather.9.cloned.1.call-start = ((), (), s32[]{:S(2)}) async-start(), calls=%async_computation.13 | async-start | bytes 4128768 | tf_op jit(solution)/shard_map/all_gather | solution.py:63
  20.4 67.0 %all-to-all-start = ((bf16[8,2,50176]{2,1,0:T(2,128)(2,1)}), bf16[8,2,50176]{2,1,0:T(2,128)(2,1)}, u32[]{:S(2)}, u32[]{:S(2)}) async-start(bf16[8,2,50176]{2,1,0:T(2,128)(2,1)} %reshape.29), calls=%async_computation | async-start | bytes 3211264 | tf_op jit(solution)/shard_map/all_to_all | solution.py:41
  26.7 362.0 %all-gather.11.cloned.1.call-start = ((), (), s32[]{:S(2)}) async-start(), calls=%async_computation.14 | async-start | bytes 4128768 | tf_op jit(solution)/shard_map/all_gather | solution.py:63
  27.5 374.5 %reduce-scatter.4.cloned.1.call-start = ((), (), s32[]{:S(2)}) async-start(), calls=%async_computation.9 | async-start | bytes 18350080 | tf_op jit(solution)/shard_map/reduce_scatter | solution.py:67
  92.1 0.7 copy-start
  171.5 316.8 %reduce-scatter.6.cloned.1.call-start = ((), (), s32[]{:S(2)}) async-start(), calls=%async_computation.10 | async-start | bytes 18350080 | tf_op jit(solution)/shard_map/reduce_scatter | solution.py:67
  290.6 338.4 %reduce-scatter.8.cloned.1.call-start = ((), (), s32[]{:S(2)}) async-start(), calls=%async_computation.11 | async-start | bytes 18350080 | tf_op jit(solution)/shard_map/reduce_scatter | solution.py:67
Sparse Core Ops, SparseCore 0:
  9.1 73.6 all-gather.6
  84.4 69.7 all-gather.8
  155.9 51.2 all-gather.10
  210.2 137.3 reduce-scatter.3
  350.5 137.7 reduce-scatter.5
  491.2 137.7 reduce-scatter.7
where the time goes:
time: 644 us; the launch traced here: 643 us
  waiting for transfers between devices  288 us (45%)
  blocking collectives  237 us (37%)
  matrix products  63.3 us (10%)
  local copies, waits for them, and re-layouts  21.5 us (3%)
  between operations  13.6 us (2%)
  other arithmetic  13 us (2%)
  starting transfers between devices  6.96 us (1%)
    reduce_scatter x3, waiting for transfers between devices, on_device(): lax.psum_scatter(partial_sum.astype(jnp.bfloat16), 'dp', scatter_dimensio...  227 us
    all_to_all x3, blocking collectives, cross_rotate(): lax.all_to_all(scaled, 'tensor', split_axis=1, concat_axis=0, tiled=True)  146 us
    all_to_all x2, blocking collectives, cross_rotate(): lax.all_to_all(stacked.astype(jnp.bfloat16), 'tensor', split_axis=0, conc...  91.1 us
    all_to_all x1, waiting for transfers between devices, cross_rotate(): lax.all_to_all(stacked.astype(jnp.bfloat16), 'tensor', split_axis=0, conc...  59.9 us
    dot_general x3, matrix products, on_device(): lax.dot_general(rotated, lax.all_gather(out_grads[seq_index], 'tensor', a...  39.4 us
    dot_general x3, matrix products, on_device(): jnp.dot(hidden_acts[seq_index], local_rot, preferred_element_type=jnp.flo...  19.2 us
    unnamed x11, local copies, waits for them, and re-layouts  17.7 us
  transfers between devices with their start and end apart: 7, of which 3 were waited for; matrix products, arithmetic and copies ran while one was open for 14% of the time, Pallas kernels for 0%

commit v1 on v0

--- a/solution.py
+++ b/solution.py
@@ -58,15 +58,15 @@
     for seq_index in range(seq_count):
         inner = jnp.dot(hidden_acts[seq_index], local_rot, preferred_element_type=jnp.float32)
         rotated = cross_rotate(inner, scaling)
-        partial_sum = lax.dot_general(
-            rotated,
-            lax.all_gather(out_grads[seq_index], "tensor", axis=1, tiled=True),
+        grads = lax.all_gather(out_grads[seq_index], "tensor", axis=1, tiled=True)
+        grads = lax.all_to_all(grads, "dp", split_axis=1, concat_axis=0, tiled=True)
+        gathered = lax.all_gather(rotated, "dp", axis=0, tiled=True)
+        summed = lax.dot_general(
+            gathered,
+            grads,
             (((0,), (0,)), ((), ())),
             preferred_element_type=jnp.float32,
         )
-        summed = lax.psum_scatter(
-            partial_sum.astype(jnp.bfloat16), "dp", scatter_dimension=1, tiled=True
-        ).astype(jnp.float32)
         gradient = summed * inv_root
         fisher = gradient * gradient if fisher is None else fisher + gradient * gradient
     return fisher / SEQS

time: 644 us -> 595 us (0.924)
  waiting for transfers between devices: 288 us -> 153 us
  blocking collectives: 237 us -> 278 us
  local copies, waits for them, and re-layouts: 21.5 us -> 59.4 us
  starting transfers between devices: 6.96 us -> 18.2 us
  other arithmetic: 13 us -> 5.64 us
    reduce_scatter x3 -> x0, waiting for transfers between devices: 227 us -> none  [on_device(): lax.psum_scatter(partial_sum.astype(jnp.bfloat16), 'dp', scatter_dimensio...]
    all_to_all x1 -> x4, waiting for transfers between devices: 59.9 us -> 151 us  [the longest x3 125 us: on_device(): grads = lax.all_to_all(grads, 'dp', split_axis=1, concat_axis=0, tiled=True)]
    all_to_all x2 -> x3, blocking collectives: 91.1 us -> 172 us  [cross_rotate(): lax.all_to_all(stacked.astype(jnp.bfloat16), 'tensor', split_axis=0, conc...]
    all_to_all x3 -> x2, blocking collectives: 146 us -> 106 us  [cross_rotate(): lax.all_to_all(scaled, 'tensor', split_axis=1, concat_axis=0, tiled=True)]
    all_to_all x0 -> x6, local copies, waits for them, and re-layouts: none -> 37.4 us  [on_device(): grads = lax.all_to_all(grads, 'dp', split_axis=1, concat_axis=0, tiled=True)]
    all_to_all x1 -> x4, starting transfers between devices: 6.35 us -> 18 us  [the longest x3 14.5 us: on_device(): grads = lax.all_to_all(grads, 'dp', split_axis=1, concat_axis=0, tiled=True)]
    div x1 -> x0, other arithmetic: 7.52 us -> none  [on_device(): return fisher / SEQS]
    unnamed x11 -> x13, local copies, waits for them, and re-layouts: 17.7 us -> 17.1 us
  transfers between devices with their start and end apart: 7 -> 10, of which waited for: 3 -> 4; matrix products, arithmetic and copies ran while one was open for 14% -> 15% of each run, Pallas kernels for 0% -> 0%
where the time goes in v1:
time: 595 us; the launch traced here: 594 us
  blocking collectives  278 us (47%)
  waiting for transfers between devices  153 us (26%)
  matrix products  65.6 us (11%)
  local copies, waits for them, and re-layouts  59.4 us (10%)
  starting transfers between devices  18.2 us (3%)
  between operations  13.7 us (2%)
    all_to_all x3, blocking collectives, cross_rotate(): lax.all_to_all(stacked.astype(jnp.bfloat16), 'tensor', split_axis=0, conc...  172 us
    all_to_all x3, waiting for transfers between devices, on_device(): grads = lax.all_to_all(grads, 'dp', split_axis=1, concat_axis=0, tiled=True)  125 us
    all_to_all x2, blocking collectives, cross_rotate(): lax.all_to_all(scaled, 'tensor', split_axis=1, concat_axis=0, tiled=True)  106 us
    dot_general x3, matrix products, on_device(): lax.dot_general(gathered, grads, (((0,), (0,)), ((), ())), preferred_elem...  41.6 us
    all_to_all x6, local copies, waits for them, and re-layouts, on_device(): grads = lax.all_to_all(grads, 'dp', split_axis=1, concat_axis=0, tiled=True)  37.4 us
    all_to_all x1, waiting for transfers between devices, cross_rotate(): lax.all_to_all(scaled, 'tensor', split_axis=1, concat_axis=0, tiled=True)  26.2 us
    dot_general x3, matrix products, on_device(): jnp.dot(hidden_acts[seq_index], local_rot, preferred_element_type=jnp.flo...  19.3 us
    unnamed x13, local copies, waits for them, and re-layouts  17.1 us
  transfers between devices with their start and end apart: 10, of which 4 were waited for; matrix products, arithmetic and copies ran while one was open for 15% of the time, Pallas kernels for 0%

profile of v1, /device:TPU:0, one launch (start us, length us, event | category | flops | bytes accessed | tf_op | source)
XLA Modules:
  0.0 594.0 jit_solution(16113864999949042203)
XLA Ops:
  6.5 0.0 all-gather.16.cloned.1.call-start
  6.5 2.4 fusion.18
  8.9 0.0 all-gather.16.cloned.1.call-update
  9.0 0.0 all-gather.18.cloned.1.call-start
  9.0 0.7 all-gather.18.cloned.1.call-update
  9.7 0.0 all-gather.20.cloned.1.call-start
  9.8 0.7 all-gather.20.cloned.1.call-update
  10.5 0.0 all-gather.10.cloned.1.call-start
  10.5 6.4 %fusion = bf16[448,1,1792]{2,0,1:T(8,128)(2,1)S(1)} fusion(bf16[1792,1792]{1,0:T(8,128)(2,1)} %constant.11.clone, bf16[3,448,1792]{2,1,0:T(8,128)(2,1)} %param.6), kind=kOutput, calls=%fused_computation.7 | convolution fusion | flops 2878095360 | bytes 9633792 | tf_op jit(solution)/shard_map/dot_general | solution.py:59
  16.9 0.5 broadcast.17
  17.4 1.9 reduce.1
  19.3 0.5 reshape.39
  19.8 67.6 %all_to_all.156 = bf16[8,2,50176]{2,1,0:T(2,128)(2,1)} all-to-all(bf16[8,2,50176]{2,1,0:T(2,128)(2,1)S(1)} %reshape.39), channel_id=1, replica_groups=mesh['dp'=4,'tensor'=8] {'tensor'}, dimensions={0} | all-to-all | bytes 3211264 | tf_op jit(solution)/shard_map/all_to_all | solution.py:41
  87.3 0.0 copy-start.1
  87.4 4.6 reshape.40
  92.0 0.2 copy.46
  92.2 0.0 copy-done.1
  92.2 1.5 fusion.3
  93.7 0.3 copy.36
  94.0 64.7 %all_to_all.157 = bf16[56,8,1792]{2,0,1:T(8,128)(2,1)} all-to-all(bf16[56,8,1792]{2,0,1:T(8,128)(2,1)S(1)} %copy.36), channel_id=1, replica_groups=mesh['dp'=4,'tensor'=8] {'tensor'}, dimensions={1} | all-to-all | bytes 3211264 | tf_op jit(solution)/shard_map/all_to_all | solution.py:46
  158.7 0.0 all-gather.10.cloned.1.call-update
  158.8 0.0 all-gather.12.cloned.1.call-start
  158.8 6.5 %fusion.1 = bf16[448,1,1792]{2,0,1:T(8,128)(2,1)S(1)} fusion(bf16[1792,1792]{1,0:T(8,128)(2,1)} %constant.11.clone, bf16[3,448,1792]{2,1,0:T(8,128)(2,1)} %param.6), kind=kOutput, calls=%fused_computation.8 | convolution fusion | flops 2878095360 | bytes 9633792 | tf_op jit(solution)/shard_map/dot_general | solution.py:59
  165.3 1.9 reduce
  167.2 0.5 reshape.37
  167.7 62.8 %all_to_all.158 = bf16[8,2,50176]{2,1,0:T(2,128)(2,1)} all-to-all(bf16[8,2,50176]{2,1,0:T(2,128)(2,1)S(1)} %reshape.37), channel_id=1, replica_groups=mesh['dp'=4,'tensor'=8] {'tensor'}, dimensions={0} | all-to-all | bytes 3211264 | tf_op jit(solution)/shard_map/all_to_all | solution.py:41
  230.4 4.7 reshape.38
  235.1 0.2 copy.47
  235.3 1.5 fusion.4
  236.9 0.3 copy.40
  237.2 41.6 %all_to_all.159 = bf16[56,8,1792]{2,0,1:T(8,128)(2,1)} all-to-all(bf16[56,8,1792]{2,0,1:T(8,128)(2,1)S(1)} %copy.40), channel_id=1, replica_groups=mesh['dp'=4,'tensor'=8] {'tensor'}, dimensions={1} | all-to-all | bytes 3211264 | tf_op jit(solution)/shard_map/all_to_all | solution.py:46
  278.8 0.0 all-gather.12.cloned.1.call-update
  278.8 6.4 %fusion.2 = bf16[448,1,1792]{2,0,1:T(8,128)(2,1)S(1)} fusion(bf16[1792,1792]{1,0:T(8,128)(2,1)} %constant.11.clone, bf16[3,448,1792]{2,1,0:T(8,128)(2,1)} %param.6), kind=kOutput, calls=%fused_computation.9 | convolution fusion | flops 2878095360 | bytes 9633792 | tf_op jit(solution)/shard_map/dot_general | solution.py:59
  285.2 1.9 reduce.2
  287.1 0.5 reshape.41
  287.6 41.6 %all_to_all.160 = bf16[8,2,50176]{2,1,0:T(2,128)(2,1)} all-to-all(bf16[8,2,50176]{2,1,0:T(2,128)(2,1)S(1)} %reshape.41), channel_id=1, replica_groups=mesh['dp'=4,'tensor'=8] {'tensor'}, dimensions={0} | all-to-all | bytes 3211264 | tf_op jit(solution)/shard_map/all_to_all | solution.py:41
  329.2 4.7 reshape.42
  333.9 0.2 copy.48
  334.1 1.5 fusion.5
  335.6 1.5 copy.44
  337.1 3.6 all-to-all-start.7
  340.7 0.0 all-gather.16.cloned.1.call-done
  340.7 7.2 %all_to_all.121 = bf16[448,4,1024]{2,1,0:T(4,128)(2,1)} reshape(bf16[1,448,4096]{2,1,0:T(8,128)(2,1)} %all-gather.16.cloned.1.call-done) | data formatting | bytes 7340032 | tf_op jit(solution)/shard_map/all_to_all | solution.py:62
  347.9 5.0 copy.37
  353.0 26.2 %all-to-all-done.7 = bf16[56,8,1792]{2,0,1:T(8,128)(2,1)S(1)} async-done(((bf16[56,8,1792]{2,0,1:T(8,128)(2,1)}), bf16[56,8,1792]{2,0,1:T(8,128)(2,1)S(1)}, u32[]{:S(2)}, u32[]{:S(2)}) %all-to-all-start.7) | async-done | bytes 1605664 | tf_op jit(solution)/shard_map/all_to_all | solution.py:46
  379.1 1.2 copy-done
  380.3 4.8 all-to-all-start.2
  385.1 0.0 all-gather.14.cloned.1.call-start
  385.1 0.5 all-gather.14.cloned.1.call-update
  385.6 0.0 all-gather.18.cloned.1.call-done
  385.7 7.2 %all_to_all.132 = bf16[448,4,1024]{2,1,0:T(4,128)(2,1)} reshape(bf16[1,448,4096]{2,1,0:T(8,128)(2,1)} %all-gather.18.cloned.1.call-done) | data formatting | bytes 7340032 | tf_op jit(solution)/shard_map/all_to_all | solution.py:62
  392.8 5.6 copy.41
  398.5 45.5 %all-to-all-done.2 = bf16[448,4,1024]{2,0,1:T(8,128)(2,1)} async-done(((bf16[448,4,1024]{2,0,1:T(8,128)(2,1)}), bf16[448,4,1024]{2,0,1:T(8,128)(2,1)}, u32[]{:S(2)}, u32[]{:S(2)}) %all-to-all-start.2) | async-done | bytes 3670048 | tf_op jit(solution)/shard_map/all_to_all | solution.py:62
  444.0 4.7 all-to-all-start.5
  448.8 0.0 all-gather.20.cloned.1.call-done
  448.8 7.3 %all_to_all.143 = bf16[448,4,1024]{2,1,0:T(4,128)(2,1)} reshape(bf16[1,448,4096]{2,1,0:T(8,128)(2,1)} %all-gather.20.cloned.1.call-done) | data formatting | bytes 7340032 | tf_op jit(solution)/shard_map/all_to_all | solution.py:62
  456.1 5.0 copy.45
  461.1 62.6 %all-to-all-done.5 = bf16[448,4,1024]{2,0,1:T(8,128)(2,1)} async-done(((bf16[448,4,1024]{2,0,1:T(8,128)(2,1)}), bf16[448,4,1024]{2,0,1:T(8,128)(2,1)}, u32[]{:S(2)}, u32[]{:S(2)}) %all-to-all-start.5) | async-done | bytes 3670048 | tf_op jit(solution)/shard_map/all_to_all | solution.py:62
  523.7 5.0 all-to-all-start.8
  528.7 0.0 all-gather.10.cloned.1.call-done
  528.8 12.3 %fusion.19 = f32[1792,1024]{1,0:T(8,128)} fusion(bf16[1792,1792]{1,0:T(8,128)(2,1)} %all-gather.10.cloned.1.call-done, bf16[1792,1024]{1,0:T(8,128)(2,1)} %bitcast.11), kind=kOutput, calls=%fused_computation.26 | convolution fusion | flops 6576668672 | bytes 17432576 | tf_op jit(solution)/shard_map/dot_general | solution.py:64
  541.1 12.3 %fusion.20 = f32[1792,1024]{1,0:T(8,128)} fusion(bf16[1792,1792]{1,0:T(8,128)(2,1)} %all-gather.12.cloned.1.call-done, bf16[1792,1024]{1,0:T(8,128)(2,1)} %bitcast.22), kind=kOutput, calls=%fused_computation.27 | convolution fusion | flops 6576668672 | bytes 17432576 | tf_op jit(solution)/shard_map/dot_general | solution.py:64
  553.4 16.8 %all-to-all-done.8 = bf16[448,4,1024]{2,0,1:T(8,128)(2,1)} async-done(((bf16[448,4,1024]{2,0,1:T(8,128)(2,1)}), bf16[448,4,1024]{2,0,1:T(8,128)(2,1)}, u32[]{:S(2)}, u32[]{:S(2)}) %all-to-all-start.8) | async-done | bytes 3670048 | tf_op jit(solution)/shard_map/all_to_all | solution.py:62
  570.1 17.0 %add_multiply_fusion = f32[1792,1024]{1,0:T(8,128)} fusion(f32[1792,1024]{1,0:T(8,128)} %fusion.20, f32[1792,1024]{1,0:T(8,128)} %fusion.19, bf16[1792,1792]{1,0:T(8,128)(2,1)} %all-gather.14.cloned.1.call-done, bf16[1792,1024]{1,0:T(8,128)(2,1)} %bitcast.33), kind=kOutput, calls=%fused_computation | convolution fusion | flops 6593183744 | bytes 32112640 | tf_op jit(solution)/shard_map/dot_general | solution.py:64
  (3 shorter events, 0.0 us)
Async XLA Ops:
  6.5 334.2 %all-gather.16.cloned.1.call-start = ((), (), s32[]{:S(2)}) async-start(), calls=%async_computation.12 | async-start | bytes 4128768 | tf_op jit(solution)/shard_map/all_gather | solution.py:61
  9.0 376.7 %all-gather.18.cloned.1.call-start = ((), (), s32[]{:S(2)}) async-start(), calls=%async_computation.13 | async-start | bytes 4128768 | tf_op jit(solution)/shard_map/all_gather | solution.py:61
  9.7 439.1 %all-gather.20.cloned.1.call-start = ((), (), s32[]{:S(2)}) async-start(), calls=%async_computation.14 | async-start | bytes 4128768 | tf_op jit(solution)/shard_map/all_gather | solution.py:61
  10.5 518.3 %all-gather.10.cloned.1.call-start = ((), (), s32[]{:S(2)}) async-start(), calls=%async_computation.9 | async-start | bytes 8028160 | tf_op jit(solution)/shard_map/all_gather | solution.py:63
  87.3 4.8 copy-start.1
  158.8 382.3 %all-gather.12.cloned.1.call-start = ((), (), s32[]{:S(2)}) async-start(), calls=%async_computation.10 | async-start | bytes 8028160 | tf_op jit(solution)/shard_map/all_gather | solution.py:63
  337.1 42.0 %all-to-all-start.7 = ((bf16[56,8,1792]{2,0,1:T(8,128)(2,1)}), bf16[56,8,1792]{2,0,1:T(8,128)(2,1)S(1)}, u32[]{:S(2)}, u32[]{:S(2)}) async-start(bf16[56,8,1792]{2,0,1:T(8,128)(2,1)} %copy.44), calls=%async_computation.7 | async-start | bytes 3211264 | tf_op jit(solution)/shard_map/all_to_all | solution.py:46
  379.1 1.2 copy-start
  380.3 63.7 %all-to-all-start.2 = ((bf16[448,4,1024]{2,0,1:T(8,128)(2,1)}), bf16[448,4,1024]{2,0,1:T(8,128)(2,1)}, u32[]{:S(2)}, u32[]{:S(2)}) async-start(bf16[448,4,1024]{2,0,1:T(8,128)(2,1)} %copy.37), calls=%async_computation.2 | async-start | bytes 7340032 | tf_op jit(solution)/shard_map/all_to_all | solution.py:62
  385.1 185.1 %all-gather.14.cloned.1.call-start = ((), (), s32[]{:S(2)}) async-start(), calls=%async_computation.11 | async-start | bytes 8028160 | tf_op jit(solution)/shard_map/all_gather | solution.py:63
  444.0 79.7 %all-to-all-start.5 = ((bf16[448,4,1024]{2,0,1:T(8,128)(2,1)}), bf16[448,4,1024]{2,0,1:T(8,128)(2,1)}, u32[]{:S(2)}, u32[]{:S(2)}) async-start(bf16[448,4,1024]{2,0,1:T(8,128)(2,1)} %copy.41), calls=%async_computation.5 | async-start | bytes 7340032 | tf_op jit(solution)/shard_map/all_to_all | solution.py:62
  523.7 46.4 %all-to-all-start.8 = ((bf16[448,4,1024]{2,0,1:T(8,128)(2,1)}), bf16[448,4,1024]{2,0,1:T(8,128)(2,1)}, u32[]{:S(2)}, u32[]{:S(2)}) async-start(bf16[448,4,1024]{2,0,1:T(8,128)(2,1)} %copy.45), calls=%async_computation.8 | async-start | bytes 7340032 | tf_op jit(solution)/shard_map/all_to_all | solution.py:62
Sparse Core Ops, SparseCore 0:
  9.1 74.0 all-gather.15
  84.8 69.8 all-gather.17
  156.3 68.9 all-gather.19
  227.0 70.0 all-gather.9
  298.7 71.0 all-gather.11
  387.4 136.4 all-gather.13

commit v2 on v1

--- a/solution.py
+++ b/solution.py
@@ -1,9 +1,12 @@
+import functools
 import math
 
 import jax
 import jax.numpy as jnp
 import numpy as np
 from jax import lax
+from jax.experimental import pallas as pl
+from jax.experimental.pallas import tpu as pltpu
 from jax.sharding import PartitionSpec as P
 
 FF = 14336
@@ -72,8 +75,315 @@
     return fisher / SEQS
 
 
+MESH = pl.DeviceIdType.MESH
+
+
+def flip(value, mask):
+    result = value
+    for bit in (1, 2, 4):
+        if mask & bit:
+            result = result + bit - 2 * bit * ((value // bit) % 2)
+    return result
+
+
+def fisher_kernel(
+    sizes, x_ref, g_ref, rot_ref, out_ref, xr, inner, mb, rot, gz, gb,
+    send_f, recv_f, send_r, recv_r, send_x, recv_x, send_y, recv_y, send_d, recv_d,
+    send_gz, recv_gz, send_gx, recv_gx, send_gp, recv_gp,
+):
+    seqs, toks, chip_rows, core_rows, scaling, inv_root = sizes
+    dpi = lax.axis_index("dp")
+    ten = lax.axis_index("tensor")
+    z, core = ten // 2, ten % 2
+    tensor_count = xr.shape[1]
+    chips = tensor_count // 2
+    dp_count = rot.shape[1] // toks
+    half = rot_ref.shape[0]
+
+    def remote(src, dst, ssem, rsem, dp_to, ten_to):
+        return pltpu.make_async_remote_copy(
+            src_ref=src, dst_ref=dst, send_sem=ssem, recv_sem=rsem,
+            device_id=(dp_to, ten_to), device_id_type=MESH,
+        )
+
+    barrier = pltpu.get_barrier_semaphore()
+    for d in range(1, tensor_count):
+        pl.semaphore_signal(barrier, inc=1, device_id=(dpi, flip(ten, d)), device_id_type=MESH)
+    for d in range(1, dp_count):
+        pl.semaphore_signal(barrier, inc=1, device_id=(flip(dpi, d), ten), device_id_type=MESH)
+    pl.semaphore_wait(barrier, tensor_count + dp_count - 2)
+
+    far_first = [d for pair in range(chips - 1, -1, -1) for d in (2 * pair, 2 * pair + 1)]
+
+    def rows_at(base, count):
+        return pl.ds(pl.multiple_of(base, 16), count)
+
+    def spread_copy(s, d, cc):
+        to_core = cc ^ (d & 1)
+        to = flip(ten, d)
+        count = core_rows[to_core]
+        base = (to // 2) * chip_rows + to_core * core_rows[0]
+        src = x_ref.at[s, rows_at(base, count)]
+        dst = xr.at[s, ten, pl.ds(0, count)]
+        if d == 0:
+            return pltpu.make_async_copy(src, dst, recv_f.at[s, 0])
+        return remote(src, dst, send_f.at[s, d], recv_f.at[s, d], dpi, to)
+
+    def start_spread(s):
+        for cc in range(2):
+            @pl.when(core == cc)
+            def _():
+                for d in far_first:
+                    spread_copy(s, d, cc).start()
+
+    def wait_spread(s):
+        for cc in range(2):
+            @pl.when(core == cc)
+            def _():
+                for d in far_first:
+                    slot = xr.at[s, flip(ten, d), pl.ds(0, core_rows[cc])]
+                    pltpu.make_async_copy(slot, slot, recv_f.at[s, d]).wait()
+
+    def mix(s):
+        for h in range(2):
+            cols = pl.ds(h * half, half)
+            block = xr[s, :, :, cols].reshape(tensor_count * core_rows[0], half)
+            inner[:, :, cols] = jnp.dot(
+                block, rot_ref[...], preferred_element_type=jnp.float32
+            ).reshape(tensor_count, core_rows[0], half)
+
+        def step(i, carry):
+            rows = rows_at((i % (core_rows[0] // 16)) * 16, 16)
+            lane = (i // (core_rows[0] // 16)) * 128
+            parts = [
+                inner[q, rows, pl.ds(pl.multiple_of(h * half + lane, 128), 128)]
+                for q in range(tensor_count) for h in range(2)
+            ]
+            stride = 1
+            while stride < len(parts):
+                mixed = list(parts)
+                for at in range(len(parts)):
+                    if at & stride == 0:
+                        mixed[at] = parts[at] + parts[at + stride]
+                        mixed[at + stride] = parts[at] - parts[at + stride]
+                parts = mixed
+                stride *= 2
+            for q in range(tensor_count):
+                for h in range(2):
+                    mb[s, q, rows, pl.ds(pl.multiple_of(h * half + lane, 128), 128)] = (
+                        parts[2 * q + h] * scaling
+                    ).astype(jnp.bfloat16)
+            return carry
+
+        lax.fori_loop(0, (core_rows[0] // 16) * (half // 128), step, 0)
+
+    def return_copy(s, d, cc):
+        to = flip(ten, d)
+        count = core_rows[cc]
+        src = mb.at[s, to, pl.ds(0, count)]
+        dst = rot.at[s, rows_at(dpi * toks + z * chip_rows + cc * core_rows[0], count)]
+        if d == 0:
+            return pltpu.make_async_copy(src, dst, recv_r.at[s, 0])
+        return remote(src, dst, send_r.at[s, d], recv_r.at[s, d], dpi, to)
+
+    def start_return(s):
+        for cc in range(2):
+            @pl.when(core == cc)
+            def _():
+                for d in [1, 0] + far_first[:-2]:
+                    return_copy(s, d, cc).start()
+
+    def chip_block(s, owner_dp, dz):
+        return rot.at[s, rows_at(owner_dp * toks + flip(z, dz) * chip_rows, chip_rows)]
+
+    def start_forward(s, dz):
+        for cc in range(2):
+            @pl.when(core == cc)
+            def _():
+                for d in (2 * dz, 2 * dz + 1):
+                    from_core = cc ^ (d & 1)
+                    piece = rot.at[s, rows_at(
+                        dpi * toks + flip(z, dz) * chip_rows + from_core * core_rows[0],
+                        core_rows[from_core],
+                    )]
+                    pltpu.make_async_copy(piece, piece, recv_r.at[s, d]).wait()
+        block = chip_block(s, dpi, dz)
+        remote(block, block, send_x.at[s, dz], recv_x.at[s, dz], flip(dpi, 1), ten).start()
+        remote(block, block, send_y.at[s, dz], recv_y.at[s, dz], flip(dpi, 2), ten).start()
+
+    def wait_block(s, owner_dp, dz, sem):
+        block = chip_block(s, owner_dp, dz)
+        pltpu.make_async_copy(block, block, sem.at[s, dz]).wait()
+
+    def start_relay(s, dz):
+        if dz % 2 == 0:
+            wait_block(s, flip(dpi, 1), dz, recv_x)
+            block, to = chip_block(s, flip(dpi, 1), dz), flip(dpi, 2)
+        else:
+            wait_block(s, flip(dpi, 2), dz, recv_y)
+            block, to = chip_block(s, flip(dpi, 2), dz), flip(dpi, 1)
+        remote(block, block, send_d.at[s, dz], recv_d.at[s, dz], to, ten).start()
+
+    def wait_rest(s):
+        for dz in dz_order:
+            if dz % 2 == 0:
+                wait_block(s, flip(dpi, 2), dz, recv_y)
+            else:
+                wait_block(s, flip(dpi, 1), dz, recv_x)
+            wait_block(s, flip(dpi, 3), dz, recv_d)
+
+    dz_order = [0] + list(range(chips - 1, 0, -1))
+
+    def gz_copy(dz):
+        if dz == 0:
+            return pltpu.make_async_copy(g_ref, gz.at[z], recv_gz.at[0])
+        return remote(g_ref, gz.at[z], send_gz.at[dz], recv_gz.at[dz], dpi, flip(ten, 2 * dz))
+
+    def grad_rows(which, owner_dp):
+        return gb.at[which, :, rows_at(owner_dp * toks, toks)]
+
+    def gx_copy(dk):
+        to = flip(dpi, dk)
+        if dk == 0:
+            return pltpu.make_async_copy(gz.at[dpi], grad_rows(core, dpi), recv_gx.at[0])
+        return remote(gz.at[to], grad_rows(core, dpi), send_gx.at[dk], recv_gx.at[dk], to, ten)
+
+    def wait_on(ref, sem):
+        pltpu.make_async_copy(ref, ref, sem).wait()
+
+    def accumulate(s):
+        tile = 256
+
+        def step(m, carry):
+            at = pl.ds(pl.multiple_of(m * tile, tile), tile)
+            left = rot[s, :, at]
+            for which in range(2):
+                width = gb.shape[-1]
+                cols = pl.ds(which * width, width)
+                gradient = lax.dot_general(
+                    left, gb[which, s], (((0,), (0,)), ((), ())),
+                    preferred_element_type=jnp.float32,
+                ) * inv_root
+                if s == 0:
+                    out_ref[at, cols] = gradient * gradient
+                elif s < seqs - 1:
+                    out_ref[at, cols] += gradient * gradient
+                else:
+                    out_ref[at, cols] = (out_ref[at, cols] + gradient * gradient) / seqs
+            return carry
+
+        lax.fori_loop(0, out_ref.shape[0] // tile, step, 0)
+
+    start_spread(0)
+    if seqs > 1:
+        start_spread(1)
+    for s in range(seqs):
+        wait_spread(s)
+        mix(s)
+        start_return(s)
+        start_forward(s, 0)
+        if s + 2 < seqs:
+            start_spread(s + 2)
+        if s == seqs - 2 or seqs == 1:
+            for dz in range(chips - 1, -1, -1):
+                gz_copy(dz).start()
+        if s >= 1:
+            for dz in dz_order[1:]:
+                start_forward(s - 1, dz)
+            for dz in dz_order:
+                start_relay(s - 1, dz)
+    for dz in range(chips):
+        wait_on(gz.at[flip(z, dz)], recv_gz.at[dz])
+    for dk in range(dp_count - 1, -1, -1):
+        gx_copy(dk).start()
+    for dk in range(dp_count):
+        block = grad_rows(core, flip(dpi, dk))
+        wait_on(block, recv_gx.at[dk])
+        remote(block, block, send_gp.at[dk], recv_gp.at[dk], dpi, flip(ten, 1)).start()
+    last = seqs - 1
+    for dk in range(dp_count):
+        wait_on(grad_rows(1 - core, flip(dpi, dk)), recv_gp.at[dk])
+    for s in range(seqs):
+        if s == last:
+            for dz in dz_order:
+                start_relay(s, dz)
+        wait_rest(s)
+        if s == max(last - 1, 0):
+            for dz in dz_order[1:]:
+                start_forward(last, dz)
+        accumulate(s)
+    for s in range(seqs):
+        for cc in range(2):
+            @pl.when(core == cc)
+            def _():
+                for d in far_first:
+                    if d:
+                        spread_copy(s, d, cc).wait_send()
+                        return_copy(s, d, cc).wait_send()
+        for dz in range(chips):
+            block = chip_block(s, dpi, dz)
+            remote(block, block, send_x.at[s, dz], recv_x.at[s, dz], flip(dpi, 1), ten).wait_send()
+            remote(block, block, send_y.at[s, dz], recv_y.at[s, dz], flip(dpi, 2), ten).wait_send()
+            remote(block, block, send_d.at[s, dz], recv_d.at[s, dz], flip(dpi, 1), ten).wait_send()
+    for dz in range(1, chips):
+        gz_copy(dz).wait_send()
+    for dk in range(dp_count):
+        if dk:
+            gx_copy(dk).wait_send()
+        block = grad_rows(core, flip(dpi, dk))
+        remote(block, block, send_gp.at[dk], recv_gp.at[dk], dpi, flip(ten, 1)).wait_send()
+
+
+def fused(hidden_acts, out_grads):
+    seqs, toks, local_ff = hidden_acts.shape
+    tensor_count, dp_count = lax.axis_size("tensor"), lax.axis_size("dp")
+    chips = tensor_count // 2
+    width = out_grads.shape[2]
+    chip_rows = toks // chips
+    first = -(-chip_rows // 32) * 16
+    core_rows = (first, chip_rows - first)
+    half = local_ff // 2
+    local_rot = jnp.asarray(np.kron(sylvester(half // FACTOR_A), paley_matrix()), jnp.bfloat16)
+    sizes = (
+        seqs, toks, chip_rows, core_rows, 1.0 / math.sqrt(FF), 1.0 / math.sqrt(toks * dp_count)
+    )
+    dma = pltpu.SemaphoreType.DMA
+    return pl.pallas_call(
+        functools.partial(fisher_kernel, sizes),
+        out_shape=jax.ShapeDtypeStruct((local_ff, 2 * width), jnp.float32),
+        in_specs=[
+            pl.BlockSpec(memory_space=pl.ANY),
+            pl.BlockSpec(memory_space=pl.ANY),
+            pl.BlockSpec(memory_space=pltpu.VMEM),
+        ],
+        out_specs=pl.BlockSpec(memory_space=pltpu.VMEM),
+        scratch_shapes=[
+            pltpu.VMEM((seqs, tensor_count, first, local_ff), jnp.bfloat16),
+            pltpu.VMEM((tensor_count, first, local_ff), jnp.float32),
+            pltpu.VMEM((seqs, tensor_count, first, local_ff), jnp.bfloat16),
+            pltpu.VMEM((seqs, toks * dp_count, local_ff), jnp.bfloat16),
+            pltpu.VMEM((chips, seqs, toks, width), jnp.bfloat16),
+            pltpu.VMEM((2, seqs, toks * dp_count, width), jnp.bfloat16),
+        ]
+        + [dma((seqs, tensor_count))] * 4
+        + [dma((seqs, chips))] * 6
+        + [dma((chips,))] * 2
+        + [dma((dp_count,))] * 4,
+        compiler_params=pltpu.CompilerParams(
+            collective_id=0, has_side_effects=True, vmem_limit_bytes=67043328
+        ),
+    )(hidden_acts, out_grads, local_rot)
+
+
+def fits_fused(mesh):
+    tensor_count, dp_count = mesh.shape["tensor"], mesh.shape["dp"]
+    local_ff = FF // tensor_count
+    return tensor_count == 8 and dp_count == 4 and local_ff % (256 * FACTOR_A // 4) == 0
+
+
 def solution(mesh):
     placed = (P(None, "dp", "tensor"), P(None, "dp", "tensor"))
+    body = fused if fits_fused(mesh) else on_device
     return jax.shard_map(
-        on_device, mesh=mesh, in_specs=placed, out_specs=P("tensor", "dp"), check_vma=False
+        body, mesh=mesh, in_specs=placed, out_specs=P("tensor", "dp"), check_vma=False
     )

time: 595 us -> 451 us (0.76)
  Pallas kernels: 0 us -> 443 us
  blocking collectives: 278 us -> 0 us
  waiting for transfers between devices: 153 us -> 0 us
  matrix products: 65.6 us -> 0 us
  local copies, waits for them, and re-layouts: 59.4 us -> 7.53 us
  starting transfers between devices: 18.2 us -> 0 us
  between operations: 13.7 us -> 0.01 us
    pallas_call x0 -> x1, Pallas kernels: none -> 443 us  [fused(): pl.pallas_call(functools.partial(fisher_kernel, sizes), out_shape=jax.Sha...]
    all_to_all x5 -> x0, blocking collectives: 278 us -> none  [the longest x3 172 us: cross_rotate(): lax.all_to_all(stacked.astype(jnp.bfloat16), 'tensor', split_axis=0, conc...]
    all_to_all x4 -> x0, waiting for transfers between devices: 151 us -> none  [the longest x3 125 us: on_device(): grads = lax.all_to_all(grads, 'dp', split_axis=1, concat_axis=0, tiled=True)]
    dot_general x9 -> x0, matrix products: 65.6 us -> none  [the longest x3 41.6 us: on_device(): lax.dot_general(gathered, grads, (((0,), (0,)), ((), ())), preferred_elem...]
    all_to_all x6 -> x0, local copies, waits for them, and re-layouts: 37.4 us -> none  [on_device(): grads = lax.all_to_all(grads, 'dp', split_axis=1, concat_axis=0, tiled=True)]
    all_to_all x4 -> x0, starting transfers between devices: 18 us -> none  [the longest x3 14.5 us: on_device(): grads = lax.all_to_all(grads, 'dp', split_axis=1, concat_axis=0, tiled=True)]
    unnamed x13 -> x1, local copies, waits for them, and re-layouts: 17.1 us -> 7.53 us
  transfers between devices with their start and end apart: 10 -> 0, of which waited for: 4 -> 0; matrix products, arithmetic and copies ran while one was open for 15% -> 0% of each run, Pallas kernels for 0% -> 0%
where the time goes in v2:
time: 451 us
  Pallas kernels  443 us (98%)
  local copies, waits for them, and re-layouts  7.53 us (2%)
    pallas_call x1, Pallas kernels, fused(): pl.pallas_call(functools.partial(fisher_kernel, sizes), out_shape=jax.Sha...  443 us

profile of v2, /device:TPU:0, one launch (start us, length us, event | category | flops | bytes accessed | tf_op | source)
XLA Modules:
  0.0 450.5 jit_solution(5937530733389399536)
XLA Ops:
  0.0 443.0 %shard_map.37 = f32[1792,1024]{1,0:T(8,128)} custom-call(bf16[3,448,1792]{2,1,0:T(8,128)(2,1)} %x_ref.1, bf16[3,448,512]{2,1,0:T(8,128)(2,1)} %g_ref.1, bf16[896,896]{1,0:T(8,128)(2,1)} %constant.2.clone.rot_ref), custom_call_target="tpu_custom_call" | custom-call | tf_op jit(solution)/shard_map/pallas_call | solution.py:351
  443.0 7.5 %copy.5 = f32[1792,1024]{1,0:T(8,128)} copy(f32[1792,1024]{1,0:T(8,128)} %shard_map.37) | data formatting | bytes 14680064

commit v3 on v2

--- a/solution.py
+++ b/solution.py
@@ -113,7 +113,7 @@
         pl.semaphore_signal(barrier, inc=1, device_id=(flip(dpi, d), ten), device_id_type=MESH)
     pl.semaphore_wait(barrier, tensor_count + dp_count - 2)
 
-    far_first = [d for pair in range(chips - 1, -1, -1) for d in (2 * pair, 2 * pair + 1)]
+    near_first = list(range(2, tensor_count)) + [1, 0]
 
     def rows_at(base, count):
         return pl.ds(pl.multiple_of(base, 16), count)
@@ -133,14 +133,14 @@
         for cc in range(2):
             @pl.when(core == cc)
             def _():
-                for d in far_first:
+                for d in near_first:
                     spread_copy(s, d, cc).start()
 
     def wait_spread(s):
         for cc in range(2):
             @pl.when(core == cc)
             def _():
-                for d in far_first:
+                for d in near_first:
                     slot = xr.at[s, flip(ten, d), pl.ds(0, core_rows[cc])]
                     pltpu.make_async_copy(slot, slot, recv_f.at[s, d]).wait()
 
@@ -190,7 +190,7 @@
         for cc in range(2):
             @pl.when(core == cc)
             def _():
-                for d in [1, 0] + far_first[:-2]:
+                for d in [1, 0] + near_first[:-2]:
                     return_copy(s, d, cc).start()
 
     def chip_block(s, owner_dp, dz):
@@ -232,21 +232,54 @@
                 wait_block(s, flip(dpi, 1), dz, recv_x)
             wait_block(s, flip(dpi, 3), dz, recv_d)
 
-    dz_order = [0] + list(range(chips - 1, 0, -1))
-
-    def gz_copy(dz):
+    dz_order = list(range(chips))
+
+    def gz_copy(s, dz):
+        src, dst, sem = g_ref.at[s], gz.at[z, s], recv_gz.at[s, dz]
         if dz == 0:
-            return pltpu.make_async_copy(g_ref, gz.at[z], recv_gz.at[0])
-        return remote(g_ref, gz.at[z], send_gz.at[dz], recv_gz.at[dz], dpi, flip(ten, 2 * dz))
-
-    def grad_rows(which, owner_dp):
-        return gb.at[which, :, rows_at(owner_dp * toks, toks)]
-
-    def gx_copy(dk):
+            return pltpu.make_async_copy(src, dst, sem)
+        return remote(src, dst, send_gz.at[s, dz], sem, dpi, flip(ten, 2 * dz))
+
+    def grad_rows(which, s, owner_dp):
+        return gb.at[which, s, rows_at(owner_dp * toks, toks)]
+
+    def gx_copy(s, dk):
         to = flip(dpi, dk)
+        src, dst, sem = gz.at[to, s], grad_rows(core, s, dpi), recv_gx.at[s, dk]
         if dk == 0:
-            return pltpu.make_async_copy(gz.at[dpi], grad_rows(core, dpi), recv_gx.at[0])
-        return remote(gz.at[to], grad_rows(core, dpi), send_gx.at[dk], recv_gx.at[dk], to, ten)
+            return pltpu.make_async_copy(src, dst, sem)
+        return remote(src, dst, send_gx.at[s, dk], sem, to, ten)
+
+    def gp_copy(s, dk):
+        block = grad_rows(core, s, flip(dpi, dk))
+        return remote(block, block, send_gp.at[s, dk], recv_gp.at[s, dk], dpi, flip(ten, 1))
+
+    def start_gz(s):
+        for dz in list(range(1, chips)) + [0]:
+            gz_copy(s, dz).start()
+
+    def start_gx(s):
+        for dz in range(chips):
+            wait_on(gz.at[flip(z, dz), s], recv_gz.at[s, dz])
+        for dk in range(dp_count - 1, -1, -1):
+            gx_copy(s, dk).start()
+
+    def start_gp(s):
+        for dk in range(dp_count):
+            wait_on(grad_rows(core, s, flip(dpi, dk)), recv_gx.at[s, dk])
+            gp_copy(s, dk).start()
+
+    def wait_grads(s):
+        for dk in range(dp_count):
+            wait_on(grad_rows(1 - core, s, flip(dpi, dk)), recv_gp.at[s, dk])
+
+    def gather(s):
+        start_relay(s, 0)
+        for dz in range(1, chips):
+            start_forward(s, dz)
+            if dz > 1:
+                start_relay(s, dz - 1)
+        start_relay(s, chips - 1)
 
     def wait_on(ref, sem):
         pltpu.make_async_copy(ref, ref, sem).wait()
@@ -274,49 +307,51 @@
 
         lax.fori_loop(0, out_ref.shape[0] // tile, step, 0)
 
-    start_spread(0)
-    if seqs > 1:
-        start_spread(1)
-    for s in range(seqs):
+    def rotate(s):
         wait_spread(s)
         mix(s)
         start_return(s)
-        start_forward(s, 0)
-        if s + 2 < seqs:
-            start_spread(s + 2)
-        if s == seqs - 2 or seqs == 1:
-            for dz in range(chips - 1, -1, -1):
-                gz_copy(dz).start()
-        if s >= 1:
-            for dz in dz_order[1:]:
-                start_forward(s - 1, dz)
-            for dz in dz_order:
-                start_relay(s - 1, dz)
-    for dz in range(chips):
-        wait_on(gz.at[flip(z, dz)], recv_gz.at[dz])
-    for dk in range(dp_count - 1, -1, -1):
-        gx_copy(dk).start()
-    for dk in range(dp_count):
-        block = grad_rows(core, flip(dpi, dk))
-        wait_on(block, recv_gx.at[dk])
-        remote(block, block, send_gp.at[dk], recv_gp.at[dk], dpi, flip(ten, 1)).start()
+
     last = seqs - 1
-    for dk in range(dp_count):
-        wait_on(grad_rows(1 - core, flip(dpi, dk)), recv_gp.at[dk])
-    for s in range(seqs):
-        if s == last:
-            for dz in dz_order:
-                start_relay(s, dz)
-        wait_rest(s)
-        if s == max(last - 1, 0):
-            for dz in dz_order[1:]:
-                start_forward(last, dz)
-        accumulate(s)
+    for s in range(last):
+        start_gz(s)
+    for s in range(last):
+        start_spread(s)
+    for s in range(last):
+        start_gx(s)
+    for s in range(last):
+        rotate(s)
+        if s == 0:
+            start_forward(0, 0)
+    start_spread(last)
+    start_gz(last)
+    for s in range(last):
+        start_gp(s)
+    for s in range(last):
+        if s:
+            start_forward(s, 0)
+        if s == last - 1:
+            for done in range(last - 1):
+                wait_grads(done)
+                wait_rest(done)
+                accumulate(done)
+        gather(s)
+    rotate(last)
+    start_forward(last, 0)
+    start_gx(last)
+    wait_grads(last - 1)
+    wait_rest(last - 1)
+    accumulate(last - 1)
+    start_gp(last)
+    gather(last)
+    wait_grads(last)
+    wait_rest(last)
+    accumulate(last)
     for s in range(seqs):
         for cc in range(2):
             @pl.when(core == cc)
             def _():
-                for d in far_first:
+                for d in near_first:
                     if d:
                         spread_copy(s, d, cc).wait_send()
                         return_copy(s, d, cc).wait_send()
@@ -325,13 +360,12 @@
             remote(block, block, send_x.at[s, dz], recv_x.at[s, dz], flip(dpi, 1), ten).wait_send()
             remote(block, block, send_y.at[s, dz], recv_y.at[s, dz], flip(dpi, 2), ten).wait_send()
             remote(block, block, send_d.at[s, dz], recv_d.at[s, dz], flip(dpi, 1), ten).wait_send()
-    for dz in range(1, chips):
-        gz_copy(dz).wait_send()
-    for dk in range(dp_count):
-        if dk:
-            gx_copy(dk).wait_send()
-        block = grad_rows(core, flip(dpi, dk))
-        remote(block, block, send_gp.at[dk], recv_gp.at[dk], dpi, flip(ten, 1)).wait_send()
+        for dz in range(1, chips):
+            gz_copy(s, dz).wait_send()
+        for dk in range(dp_count):
+            if dk:
+                gx_copy(s, dk).wait_send()
+            gp_copy(s, dk).wait_send()
 
 
 def fused(hidden_acts, out_grads):
@@ -366,9 +400,8 @@
             pltpu.VMEM((2, seqs, toks * dp_count, width), jnp.bfloat16),
         ]
         + [dma((seqs, tensor_count))] * 4
-        + [dma((seqs, chips))] * 6
-        + [dma((chips,))] * 2
-        + [dma((dp_count,))] * 4,
+        + [dma((seqs, chips))] * 8
+        + [dma((seqs, dp_count))] * 4,
         compiler_params=pltpu.CompilerParams(
             collective_id=0, has_side_effects=True, vmem_limit_bytes=67043328
         ),

time: 451 us -> 399 us (0.88)
  the two profiles are of different devices: /device:TPU:0 before, /device:TPU:8 now
where the time goes in v3:
time: 399 us; the launch traced here: 398 us
  Pallas kernels  391 us (98%)
  local copies, waits for them, and re-layouts  7.53 us (2%)
    pallas_call x1, Pallas kernels, fused(): pl.pallas_call(functools.partial(fisher_kernel, sizes), out_shape=jax.Sha...  391 us

profile of v3, /device:TPU:8, one launch (start us, length us, event | category | flops | bytes accessed | tf_op | source)
XLA Modules:
  0.0 398.4 jit_solution(9315590151074722711)
XLA Ops:
  0.0 390.8 %shard_map.37 = f32[1792,1024]{1,0:T(8,128)} custom-call(bf16[3,448,1792]{2,1,0:T(8,128)(2,1)} %x_ref.1, bf16[3,448,512]{2,1,0:T(8,128)(2,1)} %g_ref.1, bf16[896,896]{1,0:T(8,128)(2,1)} %constant.2.clone.rot_ref), custom_call_target="tpu_custom_call" | custom-call | tf_op jit(solution)/shard_map/pallas_call | solution.py:385
  390.8 7.5 %copy.5 = f32[1792,1024]{1,0:T(8,128)} copy(f32[1792,1024]{1,0:T(8,128)} %shard_map.37) | data formatting | bytes 14680064

commit v4 on v3

--- a/solution.py
+++ b/solution.py
@@ -89,7 +89,7 @@
 def fisher_kernel(
     sizes, x_ref, g_ref, rot_ref, out_ref, xr, inner, mb, rot, gz, gb,
     send_f, recv_f, send_r, recv_r, send_x, recv_x, send_y, recv_y, send_d, recv_d,
-    send_gz, recv_gz, send_gx, recv_gx, send_gp, recv_gp,
+    send_gz, recv_gz, send_gd, recv_gd, send_gx, recv_gx, send_gp, recv_gp,
 ):
     seqs, toks, chip_rows, core_rows, scaling, inv_root = sizes
     dpi = lax.axis_index("dp")
@@ -234,11 +234,35 @@
 
     dz_order = list(range(chips))
 
-    def gz_copy(s, dz):
-        src, dst, sem = g_ref.at[s], gz.at[z, s], recv_gz.at[s, dz]
-        if dz == 0:
-            return pltpu.make_async_copy(src, dst, sem)
-        return remote(src, dst, send_gz.at[s, dz], sem, dpi, flip(ten, 2 * dz))
+    def line_copy(s, hop, up):
+        own = z - hop if up else z + hop
+        src = g_ref.at[s] if hop == 0 else gz.at[own, s]
+        ssem, rsem = (send_gz, recv_gz) if up else (send_gd, recv_gd)
+        to = ten + 2 if up else ten - 2
+        return remote(src, gz.at[own, s], ssem.at[s, hop], rsem.at[s, hop + 1], dpi, to)
+
+    def line_hop(s, hop, action):
+        for up in (True, False):
+            has = z >= hop if up else z + hop < chips
+            goes_on = z + 1 < chips if up else z >= 1
+
+            if action == "start" and hop > 0:
+                @pl.when(has)
+                def _():
+                    own = z - hop if up else z + hop
+                    wait_on(gz.at[own, s], (recv_gz if up else recv_gd).at[s, hop])
+
+            if hop < chips - 1:
+                @pl.when(jnp.logical_and(has, goes_on))
+                def _():
+                    copy = line_copy(s, hop, up)
+                    if action == "start":
+                        copy.start()
+                    else:
+                        copy.wait_send()
+
+    def own_grad(s):
+        return pltpu.make_async_copy(g_ref.at[s], gz.at[z, s], recv_gz.at[s, 0])
 
     def grad_rows(which, s, owner_dp):
         return gb.at[which, s, rows_at(owner_dp * toks, toks)]
@@ -254,13 +278,8 @@
         block = grad_rows(core, s, flip(dpi, dk))
         return remote(block, block, send_gp.at[s, dk], recv_gp.at[s, dk], dpi, flip(ten, 1))
 
-    def start_gz(s):
-        for dz in list(range(1, chips)) + [0]:
-            gz_copy(s, dz).start()
-
     def start_gx(s):
-        for dz in range(chips):
-            wait_on(gz.at[flip(z, dz), s], recv_gz.at[s, dz])
+        own_grad(s).wait()
         for dk in range(dp_count - 1, -1, -1):
             gx_copy(s, dk).start()
 
@@ -313,19 +332,23 @@
         start_return(s)
 
     last = seqs - 1
-    for s in range(last):
-        start_gz(s)
+    for s in range(seqs):
+        own_grad(s).start()
+        line_hop(s, 0, "start")
+    for hop in range(1, chips - 1):
+        for s in range(seqs):
+            line_hop(s, hop, "start")
     for s in range(last):
         start_spread(s)
-    for s in range(last):
+    for s in range(seqs):
+        line_hop(s, chips - 1, "start")
         start_gx(s)
     for s in range(last):
         rotate(s)
         if s == 0:
             start_forward(0, 0)
     start_spread(last)
-    start_gz(last)
-    for s in range(last):
+    for s in range(seqs):
         start_gp(s)
     for s in range(last):
         if s:
@@ -338,11 +361,9 @@
         gather(s)
     rotate(last)
     start_forward(last, 0)
-    start_gx(last)
     wait_grads(last - 1)
     wait_rest(last - 1)
     accumulate(last - 1)
-    start_gp(last)
     gather(last)
     wait_grads(last)
     wait_rest(last)
@@ -360,8 +381,8 @@
             remote(block, block, send_x.at[s, dz], recv_x.at[s, dz], flip(dpi, 1), ten).wait_send()
             remote(block, block, send_y.at[s, dz], recv_y.at[s, dz], flip(dpi, 2), ten).wait_send()
             remote(block, block, send_d.at[s, dz], recv_d.at[s, dz], flip(dpi, 1), ten).wait_send()
-        for dz in range(1, chips):
-            gz_copy(s, dz).wait_send()
+        for hop in range(chips - 1):
+            line_hop(s, hop, "wait")
         for dk in range(dp_count):
             if dk:
                 gx_copy(s, dk).wait_send()
@@ -400,7 +421,7 @@
             pltpu.VMEM((2, seqs, toks * dp_count, width), jnp.bfloat16),
         ]
         + [dma((seqs, tensor_count))] * 4
-        + [dma((seqs, chips))] * 8
+        + [dma((seqs, chips))] * 10
         + [dma((seqs, dp_count))] * 4,
         compiler_params=pltpu.CompilerParams(
             collective_id=0, has_side_effects=True, vmem_limit_bytes=67043328

time: 399 us -> 348 us (0.87)
  the two profiles are of different devices: /device:TPU:8 before, /device:TPU:0 now
where the time goes in v4:
time: 348 us
  Pallas kernels  340 us (98%)
  local copies, waits for them, and re-layouts  7.53 us (2%)
    pallas_call x1, Pallas kernels, fused(): pl.pallas_call(functools.partial(fisher_kernel, sizes), out_shape=jax.Sha...  340 us
    unnamed x1, local copies, waits for them, and re-layouts  7.53 us

profile of v4, /device:TPU:0, one launch (start us, length us, event | category | flops | bytes accessed | tf_op | source)
XLA Modules:
  0.0 348.0 jit_solution(16655895663491939685)
XLA Ops:
  0.0 340.5 %shard_map.37 = f32[1792,1024]{1,0:T(8,128)} custom-call(bf16[3,448,1792]{2,1,0:T(8,128)(2,1)} %x_ref.1, bf16[3,448,512]{2,1,0:T(8,128)(2,1)} %g_ref.1, bf16[896,896]{1,0:T(8,128)(2,1)} %constant.2.clone.rot_ref), custom_call_target="tpu_custom_call" | custom-call | tf_op jit(solution)/shard_map/pallas_call | solution.py:406
  340.5 7.5 %copy.5 = f32[1792,1024]{1,0:T(8,128)} copy(f32[1792,1024]{1,0:T(8,128)} %shard_map.37) | data formatting | bytes 14680064
